TPU v7x, 256 devices: a whole 4x4x8 slice. The times are simulated.
256 devices in a mesh: dp: 16 (over x_hi, y, core), hid: 16 (over x_lo, z).
Axes of the slice: x: 4 (x_hi: 2, x_lo: 2; x = x_hi * 2 + x_lo), y: 4, z: 8, core: 2. Of those that a mesh axis runs over, the one named last changes fastest.
Arguments:
- tokens: bfloat16 [2048, 4096], P('dp', 'hid'), may hold values from -6 to 6
- expert_ids: int32 [2048, 2], P('dp'), may hold values from 0 to 7, all different within a row; in each aligned block of 128 rows (0 to 127, 128 to 255, ...) at most 48 rows name the same one
- gate_levels: int32 [2048, 2], P('dp'), may hold values from 1 to 255
- w_gate: bfloat16 [4096, 114688], P(None, ('dp', 'hid')), may hold values from -0.09375 to 0.09375
- w_up: bfloat16 [4096, 114688], P(None, ('dp', 'hid')), may hold values from -0.09375 to 0.09375
- w_down: bfloat16 [114688, 4096], P(('dp', 'hid')), may hold values from -0.046875 to 0.046875
Outputs:
- mixed: bfloat16 [2048, 4096], P('dp', 'hid')
Inputs may be any that keep to these rules, and one draw needn't show every extreme that they name: `expert_ids`: each row names two different experts. Among the 128 rows of one index of dp no expert is named by more than 48 rows, and in some such block one expert is named by exactly 48 rows.
All inputs are finite; a program needn't handle non-finite values.
Results may differ from a plain program's by a relative error of at most 0.019.
Values may be sent and summed in bfloat16 or wider, within the bound.
A program may use at most 64 MiB of HBM per device.

v0:
```python
import jax
import jax.numpy as jnp
from jax import lax
from jax.sharding import PartitionSpec as P

EXPERTS = 8


def local(tokens, expert_ids, gate_levels, w_gate, w_up, w_down):
    devices_dp = lax.axis_size("dp")
    halves_each = devices_dp // EXPERTS
    tok_rows = expert_ids.shape[0]
    capacity = 3 * tok_rows // 8
    flat_ids = expert_ids.reshape(-1)
    total = flat_ids.shape[0]
    one_hot = (flat_ids[:, None] == jnp.arange(EXPERTS, dtype=jnp.int32)[None, :]).astype(jnp.int32)
    earlier = jnp.cumsum(one_hot, axis=0) - one_hot
    slot_of = jnp.sum(earlier * one_hot, axis=1)
    dest_row = flat_ids * capacity + slot_of
    src_token = (
        jnp.full((EXPERTS * capacity,), -1, jnp.int32)
        .at[dest_row]
        .set(jnp.arange(total, dtype=jnp.int32) // 2)
    )
    filled = src_token >= 0
    src_index = jnp.maximum(src_token, 0)
    levels = gate_levels.astype(jnp.float32)
    gate_frac = levels / jnp.sum(levels, axis=1, keepdims=True)
    full_rows = lax.all_gather(tokens, "hid", axis=1, tiled=True)
    width = full_rows.shape[1]
    picked = jnp.where(filled[:, None], full_rows[src_index], jnp.zeros((), full_rows.dtype))
    picked = picked.reshape(EXPERTS, 1, capacity, width)
    spread = jnp.broadcast_to(picked, (EXPERTS, halves_each, capacity, width))
    received = lax.all_to_all(
        spread.reshape(devices_dp, capacity, width), "dp", split_axis=0, concat_axis=0, tiled=True
    )
    received = received.reshape(devices_dp * capacity, full_rows.shape[1])
    gate = jnp.dot(received, w_gate, preferred_element_type=jnp.float32)
    up = jnp.dot(received, w_up, preferred_element_type=jnp.float32)
    hidden = (jax.nn.silu(gate) * up).astype(jnp.bfloat16)
    partial_out = jnp.dot(hidden, w_down, preferred_element_type=jnp.float32)
    summed = lax.psum_scatter(
        partial_out.astype(jnp.bfloat16), "hid", scatter_dimension=1, tiled=True
    )
    returned = lax.all_to_all(
        summed.reshape(devices_dp, capacity, summed.shape[1]),
        "dp",
        split_axis=0,
        concat_axis=0,
        tiled=True,
    )
    halves_sum = (
        returned.reshape(EXPERTS, halves_each, capacity, summed.shape[1])
        .astype(jnp.float32)
        .sum(axis=1)
    )
    halves_sum = halves_sum.reshape(EXPERTS * capacity, summed.shape[1])
    chosen = halves_sum[dest_row] * gate_frac.reshape(-1)[:, None]
    return chosen.reshape(tok_rows, 2, summed.shape[1]).sum(axis=1).astype(jnp.bfloat16)


def solution(mesh):
    placed = (
        P("dp", "hid"),
        P("dp", None),
        P("dp", None),
        P(None, ("dp", "hid")),
        P(None, ("dp", "hid")),
        P(("dp", "hid"), None),
    )
    return jax.shard_map(
        local, mesh=mesh, in_specs=placed, out_specs=P("dp", "hid"), check_vma=False
    )
```

profile of v0, /device:TPU:1, one launch (start us, length us, event | category | flops | bytes accessed | tf_op | source)
XLA Modules:
  0.0 299.5 jit_solution(11578916369394543417)
XLA Ops:
  6.5 0.7 all-gather.2.cloned.1.call-update
  7.3 0.8 copy.9
  8.1 0.1 eq.29
  8.2 0.1 eq.25
  8.4 0.6 reduce-window.6
  9.0 0.2 slice_reduce_fusion
  9.2 0.7 broadcast_multiply_fusion
  9.9 0.1 copy.8
  10.0 0.1 mul.37
  10.3 1.4 scatter_custom_fusion
  11.8 54.8 %all-gather.2.cloned.1.call-done = bf16[128,4096]{1,0:T(8,128)(2,1)} async-done(((bf16[128,256]{1,0:T(8,128)(2,1)}), bf16[128,4096]{1,0:T(8,128)(2,1)}) %all-gather.2.cloned.1.call-update) | async-done | bytes 1048592 | tf_op jit(solution)/shard_map/all_gather | solution.py:29
  66.6 8.9 %gather_fusion = bf16[384,4096]{1,0:T(8,128)(2,1)S(1)} fusion(bf16[128,4096]{1,0:T(8,128)(2,1)} %all-gather.2.cloned.1.call-done, s32[1024]{0:T(1024)S(1)} %pad_clamp_fusion.1), kind=kCustom, calls=%fused_computation | custom fusion | bytes 6292992 | tf_op jit(solution)/shard_map/gather | solution.py:31
  75.5 0.3 broadcast_select_fusion
  75.8 0.8 broadcast_in_dim.35
  76.6 91.2 %all_to_all.10 = bf16[16,48,4096]{2,1,0:T(8,128)(2,1)S(1)} all-to-all(bf16[16,48,4096]{2,1,0:T(8,128)(2,1)S(1)} %bitcast.23), channel_id=1, replica_groups=mesh['dp'=16,'hid'=16] {'dp'}, dimensions={0} | all-to-all | bytes 12582912 | tf_op jit(solution)/shard_map/all_to_all | solution.py:34
  167.8 2.7 copy-done
  170.4 3.1 %fusion.7 = f32[768,448]{0,1:T(8,128)S(1)} fusion(bf16[768,4096]{1,0:T(8,128)(2,1)S(1)} %bitcast.26, bf16[4096,448]{0,1:T(8,128)(2,1)S(1)} %copy-done.2), kind=kOutput, calls=%fused_computation.31 | convolution fusion | flops 2818572288 | bytes 11337728 | tf_op jit(solution)/shard_map/dot_general | solution.py:38
  173.5 15.9 %convolution_convert_fusion = bf16[768,4096]{1,0:T(8,128)(2,1)} fusion(bf16[448,4096]{1,0:T(8,128)(2,1)} %param.11, bf16[768,4096]{1,0:T(8,128)(2,1)} %bitcast.27, bf16[4096,448]{0,1:T(8,128)(2,1)} %param.10, f32[768,448]{0,1:T(8,128)S(1)} %fusion.7), kind=kOutput, calls=%fused_computation.3 | convolution fusion | flops 5642354688 | bytes 21299200 | tf_op jit(solution)/shard_map/dot_general | solution.py:41
  189.5 75.5 %reduce-scatter.2.cloned.1.call-done = bf16[768,256]{1,0:T(8,128)(2,1)} async-done(((bf16[768,4096]{1,0:T(8,128)(2,1)}), bf16[768,256]{1,0:T(8,128)(2,1)}) %reduce-scatter.2.cloned.1.call-update) | async-done | bytes 393232 | tf_op jit(solution)/shard_map/reduce_scatter | solution.py:42
  264.9 15.7 %all-to-all-start.1 = ((bf16[16,48,256]{2,1,0:T(8,128)(2,1)}), bf16[16,48,256]{2,1,0:T(8,128)(2,1)S(1)}, u32[]{:S(2)}, u32[]{:S(2)}) async-start(bf16[16,48,256]{2,1,0:T(8,128)(2,1)} %bitcast.28), calls=%async_computation.2 | async-start | bytes 786432 | tf_op jit(solution)/shard_map/all_to_all | solution.py:45
  280.8 9.6 %all-to-all-done.1 = bf16[16,48,256]{2,1,0:T(8,128)(2,1)S(1)} async-done(((bf16[16,48,256]{2,1,0:T(8,128)(2,1)}), bf16[16,48,256]{2,1,0:T(8,128)(2,1)S(1)}, u32[]{:S(2)}, u32[]{:S(2)}) %all-to-all-start.1) | async-done | bytes 393248 | tf_op jit(solution)/shard_map/all_to_all | solution.py:45
  290.5 1.0 gather_fusion.1
  291.5 0.1 gather.13
  291.6 1.0 multiply_reduce_fusion
  (23 shorter events, 0.5 us)
Async XLA Ops:
  6.5 60.1 %all-gather.2.cloned.1.call-start = ((), (), s32[]{:S(2)}) async-start(), calls=%async_computation.3 | async-start | bytes 1114112 | tf_op jit(solution)/shard_map/all_gather | solution.py:29
  7.3 257.7 %reduce-scatter.2.cloned.1.call-start = ((), (), s32[]{:S(2)}) async-start(), calls=%async_computation.4 | async-start | bytes 6684672 | tf_op jit(solution)/shard_map/reduce_scatter | solution.py:42
  76.6 93.9 %copy-start.2 = (bf16[4096,448]{0,1:T(8,128)(2,1)S(1)}, bf16[4096,448]{0,1:T(8,128)(2,1)}, u32[]{:S(2)}) copy-start(bf16[4096,448]{0,1:T(8,128)(2,1)} %param.9) | copy-start | bytes 11010052
  167.8 2.7 copy-start
  189.5 91.2 %copy-start.1 = (s32[128,2]{0,1:T(2,128)S(1)}, s32[128,2]{0,1:T(2,128)}, u32[]{:S(2)}) copy-start(s32[128,2]{0,1:T(2,128)} %param.8) | copy-start | bytes 3076
  264.9 25.5 %all-to-all-start.1 = ((bf16[16,48,256]{2,1,0:T(8,128)(2,1)}), bf16[16,48,256]{2,1,0:T(8,128)(2,1)S(1)}, u32[]{:S(2)}, u32[]{:S(2)}) async-start(bf16[16,48,256]{2,1,0:T(8,128)(2,1)} %bitcast.28), calls=%async_computation.2 | async-start | bytes 786432 | tf_op jit(solution)/shard_map/all_to_all | solution.py:45
Sparse Core Ops, SparseCore 0:
  9.0 57.5 all-gather.1
  189.6 75.2 reduce-scatter.1
where the time goes:
time: 300 us; the launch traced here: 299 us
  waiting for transfers between devices  141 us (47%)
  blocking collectives  91.2 us (30%)
  matrix products  19 us (6%)
  local copies, waits for them, and re-layouts  16.6 us (6%)
  starting transfers between devices  15.8 us (5%)
  between operations  13.5 us (4%)
    all_to_all x1, blocking collectives, local(): lax.all_to_all(spread.reshape(devices_dp, capacity, width), 'dp', split_a...  91.2 us
    reduce_scatter x1, waiting for transfers between devices, local(): lax.psum_scatter(partial_out.astype(jnp.bfloat16), 'hid', scatter_dimensi...  75.5 us
    all_gather x1, waiting for transfers between devices, local(): full_rows = lax.all_gather(tokens, 'hid', axis=1, tiled=True)  54.8 us
    dot_general x1, matrix products, local(): partial_out = jnp.dot(hidden, w_down, preferred_element_type=jnp.float32)  15.9 us
    all_to_all x1, starting transfers between devices, local(): lax.all_to_all(summed.reshape(devices_dp, capacity, summed.shape[1]), 'dp...  15.7 us
    all_to_all x1, waiting for transfers between devices, local(): lax.all_to_all(summed.reshape(devices_dp, capacity, summed.shape[1]), 'dp...  9.6 us
    gather x1, local copies, waits for them, and re-layouts, local(): full_rows[src_index]  8.87 us
  transfers between devices with their start and end apart: 3, of which 3 were waited for; matrix products, arithmetic and copies ran while one was open for 2% of the time, Pallas kernels for 0%

commit v1 on v0

--- a/solution.py
+++ b/solution.py
@@ -4,6 +4,18 @@
 from jax.sharding import PartitionSpec as P
 
 EXPERTS = 8
+
+
+def end_node(mine_x):
+    return jnp.concatenate(
+        lax.all_to_all(
+            jnp.stack([mine_x for _ in range(lax.axis_size("hid"))], axis=0),
+            axis_name="hid",
+            split_axis=0,
+            concat_axis=0,
+        ),
+        axis=1,
+    )
 
 
 def local(tokens, expert_ids, gate_levels, w_gate, w_up, w_down):
@@ -26,7 +38,7 @@
     src_index = jnp.maximum(src_token, 0)
     levels = gate_levels.astype(jnp.float32)
     gate_frac = levels / jnp.sum(levels, axis=1, keepdims=True)
-    full_rows = lax.all_gather(tokens, "hid", axis=1, tiled=True)
+    full_rows = end_node(tokens)
     width = full_rows.shape[1]
     picked = jnp.where(filled[:, None], full_rows[src_index], jnp.zeros((), full_rows.dtype))
     picked = picked.reshape(EXPERTS, 1, capacity, width)

time: 300 us -> 264 us (0.88)
  waiting for transfers between devices: 141 us -> 104 us
  starting transfers between devices: 15.8 us -> 25.9 us
  blocking collectives: 91.2 us -> 82.2 us
    all_gather x1 -> x0, waiting for transfers between devices: 54.8 us -> none  [local(): full_rows = lax.all_gather(tokens, 'hid', axis=1, tiled=True)]
    all_to_all x0 -> x1, waiting for transfers between devices: none -> 21 us  [end_node(): lax.all_to_all(jnp.stack([mine_x for _ in range(lax.axis_size('hid'))], a...]
    all_to_all x0 -> x1, starting transfers between devices: none -> 10 us  [end_node(): lax.all_to_all(jnp.stack([mine_x for _ in range(lax.axis_size('hid'))], a...]
    all_to_all x1, blocking collectives: 91.2 us -> 82.2 us  [local(): lax.all_to_all(spread.reshape(devices_dp, capacity, width), 'dp', split_a...]
    gather x1, local copies, waits for them, and re-layouts: 8.87 us -> 4.04 us  [local(): full_rows[src_index]]
where the time goes in v1:
time: 264 us; the launch traced here: 263 us
  waiting for transfers between devices  104 us (39%)
  blocking collectives  82.2 us (31%)
  starting transfers between devices  25.9 us (10%)
  matrix products  19 us (7%)
  local copies, waits for them, and re-layouts  13.8 us (5%)
  between operations  13.5 us (5%)
  other arithmetic  4.72 us (2%)
    all_to_all x1, blocking collectives, local(): lax.all_to_all(spread.reshape(devices_dp, capacity, width), 'dp', split_a...  82.2 us
    reduce_scatter x1, waiting for transfers between devices, local(): lax.psum_scatter(partial_out.astype(jnp.bfloat16), 'hid', scatter_dimensi...  73.4 us
    all_to_all x1, waiting for transfers between devices, end_node(): lax.all_to_all(jnp.stack([mine_x for _ in range(lax.axis_size('hid'))], a...  21 us
    dot_general x1, matrix products, local(): partial_out = jnp.dot(hidden, w_down, preferred_element_type=jnp.float32)  15.9 us
    all_to_all x1, starting transfers between devices, local(): lax.all_to_all(summed.reshape(devices_dp, capacity, summed.shape[1]), 'dp...  15.8 us
    all_to_all x1, starting transfers between devices, end_node(): lax.all_to_all(jnp.stack([mine_x for _ in range(lax.axis_size('hid'))], a...  10 us
    all_to_all x1, waiting for transfers between devices, local(): lax.all_to_all(summed.reshape(devices_dp, capacity, summed.shape[1]), 'dp...  9.6 us
  transfers between devices with their start and end apart: 3, of which 3 were waited for; matrix products, arithmetic and copies ran while one was open for 2% of the time, Pallas kernels for 0%

profile of v1, /device:TPU:1, one launch (start us, length us, event | category | flops | bytes accessed | tf_op | source)
XLA Modules:
  0.0 263.1 jit_solution(9672616327806192865)
XLA Ops:
  6.5 1.9 stack.2
  8.5 10.0 %all-to-all-start = ((bf16[16,128,256]{2,1,0:T(8,128)(2,1)}), bf16[16,128,256]{2,1,0:T(8,128)(2,1)S(1)}, u32[]{:S(2)}, u32[]{:S(2)}) async-start(bf16[16,128,256]{2,1,0:T(8,128)(2,1)} %stack.2), calls=%async_computation | async-start | bytes 2097152 | tf_op jit(solution)/shard_map/all_to_all | solution.py:11
  18.6 0.8 copy.13
  19.3 0.1 eq.29
  19.5 0.1 eq.25
  19.6 0.6 reduce-window.6
  20.2 0.2 slice_reduce_fusion
  20.5 0.7 broadcast_multiply_fusion
  21.3 0.1 mul.37
  21.5 1.4 scatter_custom_fusion
  23.1 21.0 %all-to-all-done = bf16[16,128,256]{2,1,0:T(8,128)(2,1)S(1)} async-done(((bf16[16,128,256]{2,1,0:T(8,128)(2,1)}), bf16[16,128,256]{2,1,0:T(8,128)(2,1)S(1)}, u32[]{:S(2)}, u32[]{:S(2)}) %all-to-all-start) | async-done | bytes 1048608 | tf_op jit(solution)/shard_map/all_to_all | solution.py:11
  44.2 4.0 %gather_fusion = bf16[384,4096]{1,0:T(8,128)(2,1)} fusion(bf16[128,4096]{1,0:T(8,128)(2,1)S(1)} %bitcast.26, s32[1024]{0:T(1024)S(1)} %pad_clamp_fusion.1), kind=kCustom, calls=%fused_computation | custom fusion | bytes 6292992 | tf_op jit(solution)/shard_map/gather | solution.py:43
  48.2 2.2 broadcast_select_fusion
  50.4 0.8 broadcast_in_dim.35
  51.2 82.2 %all_to_all.15 = bf16[16,48,4096]{2,1,0:T(8,128)(2,1)S(1)} all-to-all(bf16[16,48,4096]{2,1,0:T(8,128)(2,1)S(1)} %bitcast.27), channel_id=1, replica_groups=mesh['dp'=16,'hid'=16] {'dp'}, dimensions={0} | all-to-all | bytes 12582912 | tf_op jit(solution)/shard_map/all_to_all | solution.py:46
  133.4 2.7 %copy-done = bf16[16,48,4096]{2,1,0:T(8,128)(2,1)} copy-done((bf16[16,48,4096]{2,1,0:T(8,128)(2,1)}, bf16[16,48,4096]{2,1,0:T(8,128)(2,1)S(1)}, u32[]{:S(2)}) %copy-start) | copy-done | bytes 6291480
  136.0 3.1 %fusion.7 = f32[768,448]{0,1:T(8,128)S(1)} fusion(bf16[768,4096]{1,0:T(8,128)(2,1)S(1)} %bitcast.30, bf16[4096,448]{0,1:T(8,128)(2,1)S(1)} %copy-done.2), kind=kOutput, calls=%fused_computation.31 | convolution fusion | flops 2818572288 | bytes 11337728 | tf_op jit(solution)/shard_map/dot_general | solution.py:50
  139.1 15.9 %convolution_convert_fusion = bf16[768,4096]{1,0:T(8,128)(2,1)} fusion(bf16[448,4096]{1,0:T(8,128)(2,1)} %param.11, bf16[768,4096]{1,0:T(8,128)(2,1)} %bitcast.31, bf16[4096,448]{0,1:T(8,128)(2,1)} %param.10, f32[768,448]{0,1:T(8,128)S(1)} %fusion.7), kind=kOutput, calls=%fused_computation.3 | convolution fusion | flops 5642354688 | bytes 21299200 | tf_op jit(solution)/shard_map/dot_general | solution.py:53
  155.1 73.4 %reduce-scatter.2.cloned.1.call-done = bf16[768,256]{1,0:T(8,128)(2,1)} async-done(((bf16[768,4096]{1,0:T(8,128)(2,1)}), bf16[768,256]{1,0:T(8,128)(2,1)}) %reduce-scatter.2.cloned.1.call-update) | async-done | bytes 393232 | tf_op jit(solution)/shard_map/reduce_scatter | solution.py:54
  228.5 15.8 %all-to-all-start.2 = ((bf16[16,48,256]{2,1,0:T(8,128)(2,1)}), bf16[16,48,256]{2,1,0:T(8,128)(2,1)S(1)}, u32[]{:S(2)}, u32[]{:S(2)}) async-start(bf16[16,48,256]{2,1,0:T(8,128)(2,1)} %bitcast.33), calls=%async_computation.3 | async-start | bytes 786432 | tf_op jit(solution)/shard_map/all_to_all | solution.py:57
  244.5 9.6 %all-to-all-done.2 = bf16[16,48,256]{2,1,0:T(8,128)(2,1)S(1)} async-done(((bf16[16,48,256]{2,1,0:T(8,128)(2,1)}), bf16[16,48,256]{2,1,0:T(8,128)(2,1)S(1)}, u32[]{:S(2)}, u32[]{:S(2)}) %all-to-all-start.2) | async-done | bytes 393248 | tf_op jit(solution)/shard_map/all_to_all | solution.py:57
  254.1 1.0 gather_fusion.1
  255.1 0.1 gather.13
  255.3 1.0 multiply_reduce_fusion
  (24 shorter events, 0.7 us)
Async XLA Ops:
  8.5 35.6 %all-to-all-start = ((bf16[16,128,256]{2,1,0:T(8,128)(2,1)}), bf16[16,128,256]{2,1,0:T(8,128)(2,1)S(1)}, u32[]{:S(2)}, u32[]{:S(2)}) async-start(bf16[16,128,256]{2,1,0:T(8,128)(2,1)} %stack.2), calls=%async_computation | async-start | bytes 2097152 | tf_op jit(solution)/shard_map/all_to_all | solution.py:11
  18.5 210.0 %reduce-scatter.2.cloned.1.call-start = ((), (), s32[]{:S(2)}) async-start(), calls=%async_computation.4 | async-start | bytes 6684672 | tf_op jit(solution)/shard_map/reduce_scatter | solution.py:54
  51.2 84.9 %copy-start.2 = (bf16[4096,448]{0,1:T(8,128)(2,1)S(1)}, bf16[4096,448]{0,1:T(8,128)(2,1)}, u32[]{:S(2)}) copy-start(bf16[4096,448]{0,1:T(8,128)(2,1)} %param.9) | copy-start | bytes 11010052
  133.4 2.7 %copy-start = (bf16[16,48,4096]{2,1,0:T(8,128)(2,1)}, bf16[16,48,4096]{2,1,0:T(8,128)(2,1)S(1)}, u32[]{:S(2)}) copy-start(bf16[16,48,4096]{2,1,0:T(8,128)(2,1)S(1)} %all_to_all.15) | copy-start | bytes 18874372
  155.1 89.2 %copy-start.1 = (s32[128,2]{0,1:T(2,128)S(1)}, s32[128,2]{0,1:T(2,128)}, u32[]{:S(2)}) copy-start(s32[128,2]{0,1:T(2,128)} %param.8) | copy-start | bytes 3076
  228.5 25.6 %all-to-all-start.2 = ((bf16[16,48,256]{2,1,0:T(8,128)(2,1)}), bf16[16,48,256]{2,1,0:T(8,128)(2,1)S(1)}, u32[]{:S(2)}, u32[]{:S(2)}) async-start(bf16[16,48,256]{2,1,0:T(8,128)(2,1)} %bitcast.33), calls=%async_computation.3 | async-start | bytes 786432 | tf_op jit(solution)/shard_map/all_to_all | solution.py:57
Sparse Core Ops, SparseCore 0:
  155.2 73.2 reduce-scatter.1
